TPU v7x, 512 devices: a whole 4x8x8 slice. The times are simulated.
512 devices in a mesh: rows: 64 (over z, x, core), cols: 8 (over y).
Axes of the slice: x: 4, y: 8, z: 8, core: 2. Of those that a mesh axis runs over, the one named last changes fastest.
Arguments:
- rhs: float32 [3, 128, 256, 128], P(None, 'rows', 'cols'), may hold values from -6 to 6
- diag_inv: float32 [3, 128, 256, 256], P(None, 'rows', 'cols'), may hold values from -1 to 3.1, as said below
- factor_tiles: float32 [2, 128, 8, 256, 256], P(None, 'rows', None, 'cols'), may hold values from -0.125 to 0.125
- tile_source: int32 [2, 128, 8], P(None, 'rows'), may hold values from 0 to 255, as said below
- tile_count: int32 [2, 128], P(None, 'rows'), may hold values from 1 to 8, as said below
Outputs:
- solution: float32 [3, 128, 256, 128], P(None, 'rows', 'cols')
Inputs may be any that keep to these rules, and one draw needn't show every extreme that they name: `tile_source`: each source lies at a lower level than its target; supernode g mod 128 belongs to rows index (g mod 128) // 2, and that index differs from the target's by at most 7. The 8 sources of one supernode are distinct. `tile_count`: slots at or beyond the count hold no tile of the factor. At every target level some supernode has all 8 slots live. `diag_inv`: each block is lower triangular with a positive diagonal.
All inputs are finite; a program needn't handle non-finite values.
Results may differ from a plain program's by a relative error of at most 0.0003.
Values sent between devices are 32-bit elements; how exact they have to be, the bound alone decides.
A program may use at most 64 MiB of HBM per device.

v0:
```python
import jax
import jax.numpy as jnp
from jax import lax
from jax.sharding import PartitionSpec as P

KDEV = 7


def from_behind(value, axis, steps):
    count = lax.axis_size(axis)
    leading, last = (max(0, -steps), min(count, count - steps))
    return lax.ppermute(value, axis, [(source, source + steps) for source in range(leading, last)])


def local(rhs, diag_inv, factor_tiles, tile_source, tile_count):
    levels = rhs.shape[0]
    owned_count = rhs.shape[1]
    share_rows = rhs.shape[2]
    columns = rhs.shape[3]
    slot_count = tile_source.shape[2]
    reach_dev = KDEV
    window_len = 2 * reach_dev + 1
    total_sup = lax.axis_size("rows") * owned_count
    row_place = lax.axis_index("rows")
    highest = lax.Precision.HIGHEST
    slot_ids = jnp.arange(slot_count, dtype=jnp.int32)

    def window_places(sources):
        src_level = sources // total_sup
        within = sources % total_sup
        return (
            src_level * window_len + within // owned_count - row_place + reach_dev
        ) * owned_count + within % owned_count

    def live_mask(counts):
        return (slot_ids[None, :] < counts[:, None]).astype(jnp.float32)

    def full_rows(piece):
        return lax.all_gather(piece, "cols", axis=1, tiled=True)

    forward_values = []
    windows = []
    for height in range(levels):
        if height == 0:
            whole_block = full_rows(rhs[0])
        else:
            stacked = jnp.stack(windows, 0).reshape(
                height * window_len * owned_count, share_rows, columns
            )
            places = window_places(tile_source[height - 1])
            picked = (
                jnp.take(stacked, places, axis=0)
                * live_mask(tile_count[height - 1])[:, :, None, None]
            )
            partial_value = jnp.einsum(
                "skci,skcr->sir", factor_tiles[height - 1], picked, precision=highest
            )
            whole_block = full_rows(
                rhs[height]
                - lax.psum_scatter(partial_value, "cols", scatter_dimension=1, tiled=True)
            )
        values = jnp.einsum("sci,sir->scr", diag_inv[height], whole_block, precision=highest)
        forward_values.append(values)
        if height + 1 < levels:
            pieces = []
            for pull_offset in range(-reach_dev, reach_dev + 1):
                if pull_offset == 0:
                    pieces.append(values)
                else:
                    pieces.append(from_behind(values, "rows", -pull_offset))
            windows.append(jnp.stack(pieces, 0))
    carried = [jnp.zeros_like(forward_values[0]) for height in range(levels)]
    solution = [None] * levels
    for height in reversed(range(levels)):
        partial_value = jnp.einsum(
            "sci,scr->sir",
            diag_inv[height],
            forward_values[height] - carried[height],
            precision=highest,
        )
        own_share = lax.psum_scatter(partial_value, "cols", scatter_dimension=1, tiled=True)
        if height > 0:
            whole_block = lax.all_gather(own_share, "cols", axis=1, tiled=True)
        solution[height] = own_share
        if height > 0:
            term_set = jnp.einsum(
                "skci,sir->skcr", factor_tiles[height - 1], whole_block, precision=highest
            )
            term_set = term_set * live_mask(tile_count[height - 1])[:, :, None, None]
            places = window_places(tile_source[height - 1]).reshape(-1)
            targets = height * window_len * owned_count
            one_hot = (jnp.arange(targets, dtype=jnp.int32)[:, None] == places[None, :]).astype(
                jnp.float32
            )
            outgoing = jnp.einsum(
                "ms,slg->mlg",
                one_hot,
                term_set.reshape(owned_count * slot_count, share_rows, columns),
                precision=highest,
            )
            push_outgoing = outgoing.reshape(height, window_len, owned_count, share_rows, columns)
            received = push_outgoing[:, reach_dev]
            for offset in range(-reach_dev, reach_dev + 1):
                if offset != 0:
                    received = received + from_behind(
                        push_outgoing[:, reach_dev + offset], "rows", offset
                    )
            for lower_level in range(height):
                carried[lower_level] = carried[lower_level] + received[lower_level]
    return jnp.stack(solution, 0)


def solution(mesh):
    placed = (
        P(None, "rows", "cols", None),
        P(None, "rows", "cols", None),
        P(None, "rows", None, "cols", None),
        P(None, "rows", None),
        P(None, "rows"),
    )
    return jax.shard_map(
        local, mesh=mesh, in_specs=placed, out_specs=P(None, "rows", "cols", None), check_vma=False
    )
```

profile of v0, /device:TPU:2, one launch (start us, length us, event | category | flops | bytes accessed | tf_op | source)
XLA Modules:
  0.0 670.9 jit_solution(4755036083736061673)
XLA Ops:
  7.3 26.5 %all-gather = f32[1,2,256,128]{3,2,1,0:T(8,128)S(1)} all-gather(f32[1,2,32,128]{3,2,1,0:T(8,128)S(1)} %slice-done), channel_id=2, replica_groups=mesh['rows'=64,'cols'=8] {'cols'}, dimensions={2}, use_global_device_ids=true | all-gather | bytes 294912 | tf_op jit(solution)/shard_map/all_gather | solution.py:39
  35.4 4.9 collective-permute-start.1
  40.2 6.1 collective-permute-start.2
  46.4 4.8 collective-permute-start.3
  52.7 4.0 collective-permute-start.5
  56.8 4.5 collective-permute-start.6
  61.3 1.9 collective-permute-start.7
  63.2 1.9 collective-permute-start.8
  71.8 3.7 collective-permute-done.10
  77.1 4.2 collective-permute-done.12
  83.4 1.8 convolution_bitcast_fusion.1
  85.4 44.6 %reduce-scatter.3.cloned.1.call-done = f32[2,32,128]{2,1,0:T(8,128)} async-done(((f32[2,256,128]{2,1,0:T(8,128)}), f32[2,32,128]{2,1,0:T(8,128)}) %reduce-scatter.3.cloned.1.call-update) | async-done | bytes 32784 | tf_op jit(solution)/shard_map/reduce_scatter | solution.py:60
  130.9 24.8 %all_gather.16 = f32[2,256,128]{2,1,0:T(8,128)S(1)} all-gather(f32[2,32,128]{2,1,0:T(8,128)S(1)} %bitcast_subtract_fusion), channel_id=1, replica_groups=mesh['rows'=64,'cols'=8] {'cols'}, dimensions={1}, use_global_device_ids=true | all-gather | bytes 294912 | tf_op jit(solution)/shard_map/all_gather | solution.py:39
  157.2 4.2 collective-permute-start.15
  161.4 5.4 collective-permute-start.16
  166.8 4.1 collective-permute-start.17
  172.7 3.8 collective-permute-start.19
  176.5 4.2 collective-permute-start.20
  180.7 1.9 collective-permute-start.21
  182.7 1.9 collective-permute-start.22
  191.3 3.0 collective-permute-done.24
  195.9 4.2 collective-permute-done.26
  202.2 1.8 convolution_bitcast_fusion
  204.1 43.1 %reduce-scatter.5.cloned.1.call-done = f32[2,32,128]{2,1,0:T(8,128)} async-done(((f32[2,256,128]{2,1,0:T(8,128)}), f32[2,32,128]{2,1,0:T(8,128)}) %reduce-scatter.5.cloned.1.call-update) | async-done | bytes 32784 | tf_op jit(solution)/shard_map/reduce_scatter | solution.py:60
  248.0 24.8 %all_gather.17 = f32[2,256,128]{2,1,0:T(8,128)S(1)} all-gather(f32[2,32,128]{2,1,0:T(8,128)S(1)} %bitcast_subtract_fusion.1), channel_id=1, replica_groups=mesh['rows'=64,'cols'=8] {'cols'}, dimensions={1}, use_global_device_ids=true | all-gather | bytes 294912 | tf_op jit(solution)/shard_map/all_gather | solution.py:39
  276.5 74.7 %all-reduce.7.cloned.1.call-done = f32[2,256,128]{2,0,1:T(2,128)} async-done(((f32[2,256,128]{2,0,1:T(2,128)}), f32[2,256,128]{2,0,1:T(2,128)}) %all-reduce.7.cloned.1.call-update) | async-done | bytes 262160
  351.9 24.9 %all_gather.18 = f32[2,256,128]{2,0,1:T(2,128)S(1)} all-gather(f32[2,32,128]{2,0,1:T(2,128)S(1)} %constant_dynamic-slice_fusion.1), channel_id=1, replica_groups=mesh['rows'=64,'cols'=8] {'cols'}, dimensions={1}, use_global_device_ids=true | all-gather | bytes 294912 | tf_op jit(solution)/shard_map/all_gather | solution.py:83
  380.3 4.2 collective-permute-start.40
  384.5 5.4 collective-permute-start.39
  389.8 4.1 collective-permute-start.38
  395.8 3.7 collective-permute-start.36
  399.5 4.3 collective-permute-start.35
  403.8 1.9 collective-permute-start.34
  405.7 1.9 collective-permute-start.33
  414.2 3.8 collective-permute-done.31
  419.2 4.4 collective-permute-done.29
  426.6 81.3 %all-reduce.9.cloned.1.call-done = f32[2,256,128]{2,0,1:T(2,128)} async-done(((f32[2,256,128]{2,0,1:T(2,128)}), f32[2,256,128]{2,0,1:T(2,128)}) %all-reduce.9.cloned.1.call-update) | async-done | bytes 262160
  508.6 24.9 %all_gather.19 = f32[2,256,128]{2,0,1:T(2,128)S(1)} all-gather(f32[2,32,128]{2,0,1:T(2,128)S(1)} %constant_dynamic-slice_fusion), channel_id=1, replica_groups=mesh['rows'=64,'cols'=8] {'cols'}, dimensions={1}, use_global_device_ids=true | all-gather | bytes 294912 | tf_op jit(solution)/shard_map/all_gather | solution.py:83
  536.1 4.2 collective-permute-start.54
  540.3 5.4 collective-permute-start.53
  545.7 4.2 collective-permute-start.52
  551.6 3.7 collective-permute-start.50
  555.3 4.3 collective-permute-start.49
  559.6 1.9 collective-permute-start.48
  561.5 1.9 collective-permute-start.47
  570.0 3.1 collective-permute-done.45
  574.7 4.2 collective-permute-done.43
  583.2 79.8 %all-reduce.11.cloned.1.call-done = f32[2,256,128]{2,0,1:T(2,128)} async-done(((f32[2,256,128]{2,0,1:T(2,128)}), f32[2,256,128]{2,0,1:T(2,128)}) %all-reduce.11.cloned.1.call-update) | async-done | bytes 262160
  (174 shorter events, 67.9 us)
Async XLA Ops:
  6.5 123.5 %reduce-scatter.3.cloned.1.call-start = ((), (), s32[]{:S(2)}) async-start(), calls=%async_computation.2 | async-start | bytes 294912 | tf_op jit(solution)/shard_map/reduce_scatter | solution.py:60
  34.1 18.7 %collective-permute-start = (f32[2,32,128]{2,1,0:T(8,128)S(1)}, f32[2,32,128]{2,1,0:T(8,128)S(1)}, u32[]{:S(2)}, u32[]{:S(2)}) collective-permute-start(f32[2,32,128]{2,1,0:T(8,128)S(1)} %fusion.14), channel_id=1, source_target_pairs={{0,56},{8,64},{16,72},{24,80},{32,88},{40,96},{48,104},{56,112},{6... | collective-permute-start | bytes 98312 | tf_op jit(solution)/shard_map/ppermute | solution.py:12
  35.4 21.4 %collective-permute-start.1 = (f32[2,32,128]{2,1,0:T(8,128)S(1)}, f32[2,32,128]{2,1,0:T(8,128)S(1)}, u32[]{:S(2)}, u32[]{:S(2)}) collective-permute-start(f32[2,32,128]{2,1,0:T(8,128)S(1)} %fusion.14), channel_id=1, source_target_pairs={{0,48},{8,56},{16,64},{24,72},{32,80},{40,88},{48,96},{56,104},{64... | collective-permute-start | bytes 98312 | tf_op jit(solution)/shard_map/ppermute | solution.py:12
  40.2 21.0 %collective-permute-start.2 = (f32[2,32,128]{2,1,0:T(8,128)S(1)}, f32[2,32,128]{2,1,0:T(8,128)S(1)}, u32[]{:S(2)}, u32[]{:S(2)}) collective-permute-start(f32[2,32,128]{2,1,0:T(8,128)S(1)} %fusion.14), channel_id=1, source_target_pairs={{0,40},{8,48},{16,56},{24,64},{32,72},{40,80},{48,88},{56,96},{64,... | collective-permute-start | bytes 98312 | tf_op jit(solution)/shard_map/ppermute | solution.py:12
  46.4 16.9 %collective-permute-start.3 = (f32[2,32,128]{2,1,0:T(8,128)S(1)}, f32[2,32,128]{2,1,0:T(8,128)S(1)}, u32[]{:S(2)}, u32[]{:S(2)}) collective-permute-start(f32[2,32,128]{2,1,0:T(8,128)S(1)} %fusion.14), channel_id=1, source_target_pairs={{0,32},{8,40},{16,48},{24,56},{32,64},{40,72},{48,80},{56,88},{64,... | collective-permute-start | bytes 98312 | tf_op jit(solution)/shard_map/ppermute | solution.py:12
  51.2 14.0 %collective-permute-start.4 = (f32[2,32,128]{2,1,0:T(8,128)S(1)}, f32[2,32,128]{2,1,0:T(8,128)S(1)}, u32[]{:S(2)}, u32[]{:S(2)}) collective-permute-start(f32[2,32,128]{2,1,0:T(8,128)S(1)} %fusion.14), channel_id=1, source_target_pairs={{0,24},{8,32},{16,40},{24,48},{32,56},{40,64},{48,72},{56,80},{64,... | collective-permute-start | bytes 98312 | tf_op jit(solution)/shard_map/ppermute | solution.py:12
  52.7 13.8 %collective-permute-start.5 = (f32[2,32,128]{2,1,0:T(8,128)S(1)}, f32[2,32,128]{2,1,0:T(8,128)S(1)}, u32[]{:S(2)}, u32[]{:S(2)}) collective-permute-start(f32[2,32,128]{2,1,0:T(8,128)S(1)} %fusion.14), channel_id=1, source_target_pairs={{0,16},{8,24},{16,32},{24,40},{32,48},{40,56},{48,64},{56,72},{64,... | collective-permute-start | bytes 98312 | tf_op jit(solution)/shard_map/ppermute | solution.py:12
  56.8 11.0 %collective-permute-start.6 = (f32[2,32,128]{2,1,0:T(8,128)S(1)}, f32[2,32,128]{2,1,0:T(8,128)S(1)}, u32[]{:S(2)}, u32[]{:S(2)}) collective-permute-start(f32[2,32,128]{2,1,0:T(8,128)S(1)} %fusion.14), channel_id=1, source_target_pairs={{0,8},{8,16},{16,24},{24,32},{32,40},{40,48},{48,56},{56,64},{64,7... | collective-permute-start | bytes 98312 | tf_op jit(solution)/shard_map/ppermute | solution.py:12
  66.5 9.0 %collective-permute-start.10 = (f32[2,32,128]{2,1,0:T(8,128)S(1)}, f32[2,32,128]{2,1,0:T(8,128)S(1)}, u32[]{:S(2)}, u32[]{:S(2)}) collective-permute-start(f32[2,32,128]{2,1,0:T(8,128)S(1)} %fusion.14), channel_id=1, source_target_pairs={{32,0},{40,8},{48,16},{56,24},{64,32},{72,40},{80,48},{88,56},{96,... | collective-permute-start | bytes 98312 | tf_op jit(solution)/shard_map/ppermute | solution.py:12
  67.8 9.3 %collective-permute-start.11 = (f32[2,32,128]{2,1,0:T(8,128)S(1)}, f32[2,32,128]{2,1,0:T(8,128)S(1)}, u32[]{:S(2)}, u32[]{:S(2)}) collective-permute-start(f32[2,32,128]{2,1,0:T(8,128)S(1)} %fusion.14), channel_id=1, source_target_pairs={{40,0},{48,8},{56,16},{64,24},{72,32},{80,40},{88,48},{96,56},{104... | collective-permute-start | bytes 98312 | tf_op jit(solution)/shard_map/ppermute | solution.py:12
  69.2 12.2 %collective-permute-start.12 = (f32[2,32,128]{2,1,0:T(8,128)S(1)}, f32[2,32,128]{2,1,0:T(8,128)S(1)}, u32[]{:S(2)}, u32[]{:S(2)}) collective-permute-start(f32[2,32,128]{2,1,0:T(8,128)S(1)} %fusion.14), channel_id=1, source_target_pairs={{48,0},{56,8},{64,16},{72,24},{80,32},{88,40},{96,48},{104,56},{11... | collective-permute-start | bytes 98312 | tf_op jit(solution)/shard_map/ppermute | solution.py:12
  70.5 12.3 %collective-permute-start.13 = (f32[2,32,128]{2,1,0:T(8,128)S(1)}, f32[2,32,128]{2,1,0:T(8,128)S(1)}, u32[]{:S(2)}, u32[]{:S(2)}) collective-permute-start(f32[2,32,128]{2,1,0:T(8,128)S(1)} %fusion.14), channel_id=1, source_target_pairs={{56,0},{64,8},{72,16},{80,24},{88,32},{96,40},{104,48},{112,56},{1... | collective-permute-start | bytes 98312 | tf_op jit(solution)/shard_map/ppermute | solution.py:12
  85.2 162.0 %reduce-scatter.5.cloned.1.call-start = ((), (), s32[]{:S(2)}) async-start(), calls=%async_computation.3 | async-start | bytes 294912 | tf_op jit(solution)/shard_map/reduce_scatter | solution.py:60
  155.9 16.8 %collective-permute-start.14 = (f32[2,32,128]{2,1,0:T(8,128)S(1)}, f32[2,32,128]{2,1,0:T(8,128)S(1)}, u32[]{:S(2)}, u32[]{:S(2)}) collective-permute-start(f32[2,32,128]{2,1,0:T(8,128)S(1)} %bitcast.360), channel_id=1, source_target_pairs={{0,56},{8,64},{16,72},{24,80},{32,88},{40,96},{48,104},{56,112},{6... | collective-permute-start | bytes 98312 | tf_op jit(solution)/shard_map/ppermute | solution.py:12
  157.2 19.3 %collective-permute-start.15 = (f32[2,32,128]{2,1,0:T(8,128)S(1)}, f32[2,32,128]{2,1,0:T(8,128)S(1)}, u32[]{:S(2)}, u32[]{:S(2)}) collective-permute-start(f32[2,32,128]{2,1,0:T(8,128)S(1)} %bitcast.361), channel_id=1, source_target_pairs={{0,48},{8,56},{16,64},{24,72},{32,80},{40,88},{48,96},{56,104},{64... | collective-permute-start | bytes 98312 | tf_op jit(solution)/shard_map/ppermute | solution.py:12
  161.4 19.3 %collective-permute-start.16 = (f32[2,32,128]{2,1,0:T(8,128)S(1)}, f32[2,32,128]{2,1,0:T(8,128)S(1)}, u32[]{:S(2)}, u32[]{:S(2)}) collective-permute-start(f32[2,32,128]{2,1,0:T(8,128)S(1)} %bitcast.362), channel_id=1, source_target_pairs={{0,40},{8,48},{16,56},{24,64},{32,72},{40,80},{48,88},{56,96},{64,... | collective-permute-start | bytes 98312 | tf_op jit(solution)/shard_map/ppermute | solution.py:12
  166.8 15.9 %collective-permute-start.17 = (f32[2,32,128]{2,1,0:T(8,128)S(1)}, f32[2,32,128]{2,1,0:T(8,128)S(1)}, u32[]{:S(2)}, u32[]{:S(2)}) collective-permute-start(f32[2,32,128]{2,1,0:T(8,128)S(1)} %bitcast.363), channel_id=1, source_target_pairs={{0,32},{8,40},{16,48},{24,56},{32,64},{40,72},{48,80},{56,88},{64,... | collective-permute-start | bytes 98312 | tf_op jit(solution)/shard_map/ppermute | solution.py:12
  170.9 13.7 %collective-permute-start.18 = (f32[2,32,128]{2,1,0:T(8,128)S(1)}, f32[2,32,128]{2,1,0:T(8,128)S(1)}, u32[]{:S(2)}, u32[]{:S(2)}) collective-permute-start(f32[2,32,128]{2,1,0:T(8,128)S(1)} %bitcast.364), channel_id=1, source_target_pairs={{0,24},{8,32},{16,40},{24,48},{32,56},{40,64},{48,72},{56,80},{64,... | collective-permute-start | bytes 98312 | tf_op jit(solution)/shard_map/ppermute | solution.py:12
  172.7 13.2 %collective-permute-start.19 = (f32[2,32,128]{2,1,0:T(8,128)S(1)}, f32[2,32,128]{2,1,0:T(8,128)S(1)}, u32[]{:S(2)}, u32[]{:S(2)}) collective-permute-start(f32[2,32,128]{2,1,0:T(8,128)S(1)} %bitcast.365), channel_id=1, source_target_pairs={{0,16},{8,24},{16,32},{24,40},{32,48},{40,56},{48,64},{56,72},{64,... | collective-permute-start | bytes 98312 | tf_op jit(solution)/shard_map/ppermute | solution.py:12
  176.5 10.7 %collective-permute-start.20 = (f32[2,32,128]{2,1,0:T(8,128)S(1)}, f32[2,32,128]{2,1,0:T(8,128)S(1)}, u32[]{:S(2)}, u32[]{:S(2)}) collective-permute-start(f32[2,32,128]{2,1,0:T(8,128)S(1)} %bitcast.366), channel_id=1, source_target_pairs={{0,8},{8,16},{16,24},{24,32},{32,40},{40,48},{48,56},{56,64},{64,7... | collective-permute-start | bytes 98312 | tf_op jit(solution)/shard_map/ppermute | solution.py:12
  185.9 8.3 %collective-permute-start.24 = (f32[2,32,128]{2,1,0:T(8,128)S(1)}, f32[2,32,128]{2,1,0:T(8,128)S(1)}, u32[]{:S(2)}, u32[]{:S(2)}) collective-permute-start(f32[2,32,128]{2,1,0:T(8,128)S(1)} %bitcast.370), channel_id=1, source_target_pairs={{32,0},{40,8},{48,16},{56,24},{64,32},{72,40},{80,48},{88,56},{96,... | collective-permute-start | bytes 98312 | tf_op jit(solution)/shard_map/ppermute | solution.py:12
  187.3 8.6 %collective-permute-start.25 = (f32[2,32,128]{2,1,0:T(8,128)S(1)}, f32[2,32,128]{2,1,0:T(8,128)S(1)}, u32[]{:S(2)}, u32[]{:S(2)}) collective-permute-start(f32[2,32,128]{2,1,0:T(8,128)S(1)} %bitcast.371), channel_id=1, source_target_pairs={{40,0},{48,8},{56,16},{64,24},{72,32},{80,40},{88,48},{96,56},{104... | collective-permute-start | bytes 98312 | tf_op jit(solution)/shard_map/ppermute | solution.py:12
  188.6 11.5 %collective-permute-start.26 = (f32[2,32,128]{2,1,0:T(8,128)S(1)}, f32[2,32,128]{2,1,0:T(8,128)S(1)}, u32[]{:S(2)}, u32[]{:S(2)}) collective-permute-start(f32[2,32,128]{2,1,0:T(8,128)S(1)} %bitcast.372), channel_id=1, source_target_pairs={{48,0},{56,8},{64,16},{72,24},{80,32},{88,40},{96,48},{104,56},{11... | collective-permute-start | bytes 98312 | tf_op jit(solution)/shard_map/ppermute | solution.py:12
  189.9 11.6 %collective-permute-start.27 = (f32[2,32,128]{2,1,0:T(8,128)S(1)}, f32[2,32,128]{2,1,0:T(8,128)S(1)}, u32[]{:S(2)}, u32[]{:S(2)}) collective-permute-start(f32[2,32,128]{2,1,0:T(8,128)S(1)} %bitcast.373), channel_id=1, source_target_pairs={{56,0},{64,8},{72,16},{80,24},{88,32},{96,40},{104,48},{112,56},{1... | collective-permute-start | bytes 98312 | tf_op jit(solution)/shard_map/ppermute | solution.py:12
  204.1 147.1 %all-reduce.7.cloned.1.call-start = ((), (), s32[]{:S(2)}) async-start(), calls=%async_computation.4 | async-start | bytes 524288
  274.3 233.6 %all-reduce.9.cloned.1.call-start = ((), (), s32[]{:S(2)}) async-start(), calls=%async_computation.5 | async-start | bytes 524288
  379.0 16.8 %collective-permute-start.41 = (f32[2,2,32,128]{3,2,1,0:T(8,128)S(1)}, f32[2,2,32,128]{3,2,1,0:T(8,128)S(1)}, u32[]{:S(2)}, u32[]{:S(2)}) collective-permute-start(f32[2,2,32,128]{3,2,1,0:T(8,128)S(1)} %bitcast.388), channel_id=1, source_target_pairs={{0,56},{8,64},{16,72},{24,80},{32,88},{40,96},{48,104},{56,112},{6... | collective-permute-start | bytes 196616 | tf_op jit(solution)/shard_map/ppermute | solution.py:12
  380.3 19.2 %collective-permute-start.40 = (f32[2,2,32,128]{3,2,1,0:T(8,128)S(1)}, f32[2,2,32,128]{3,2,1,0:T(8,128)S(1)}, u32[]{:S(2)}, u32[]{:S(2)}) collective-permute-start(f32[2,2,32,128]{3,2,1,0:T(8,128)S(1)} %bitcast.387), channel_id=1, source_target_pairs={{0,48},{8,56},{16,64},{24,72},{32,80},{40,88},{48,96},{56,104},{64... | collective-permute-start | bytes 196616 | tf_op jit(solution)/shard_map/ppermute | solution.py:12
  384.5 19.3 %collective-permute-start.39 = (f32[2,2,32,128]{3,2,1,0:T(8,128)S(1)}, f32[2,2,32,128]{3,2,1,0:T(8,128)S(1)}, u32[]{:S(2)}, u32[]{:S(2)}) collective-permute-start(f32[2,2,32,128]{3,2,1,0:T(8,128)S(1)} %bitcast.386), channel_id=1, source_target_pairs={{0,40},{8,48},{16,56},{24,64},{32,72},{40,80},{48,88},{56,96},{64,... | collective-permute-start | bytes 196616 | tf_op jit(solution)/shard_map/ppermute | solution.py:12
  389.8 15.9 %collective-permute-start.38 = (f32[2,2,32,128]{3,2,1,0:T(8,128)S(1)}, f32[2,2,32,128]{3,2,1,0:T(8,128)S(1)}, u32[]{:S(2)}, u32[]{:S(2)}) collective-permute-start(f32[2,2,32,128]{3,2,1,0:T(8,128)S(1)} %bitcast.385), channel_id=1, source_target_pairs={{0,32},{8,40},{16,48},{24,56},{32,64},{40,72},{48,80},{56,88},{64,... | collective-permute-start | bytes 196616 | tf_op jit(solution)/shard_map/ppermute | solution.py:12
  394.0 13.6 %collective-permute-start.37 = (f32[2,2,32,128]{3,2,1,0:T(8,128)S(1)}, f32[2,2,32,128]{3,2,1,0:T(8,128)S(1)}, u32[]{:S(2)}, u32[]{:S(2)}) collective-permute-start(f32[2,2,32,128]{3,2,1,0:T(8,128)S(1)} %bitcast.384), channel_id=1, source_target_pairs={{0,24},{8,32},{16,40},{24,48},{32,56},{40,64},{48,72},{56,80},{64,... | collective-permute-start | bytes 196616 | tf_op jit(solution)/shard_map/ppermute | solution.py:12
  395.8 13.2 %collective-permute-start.36 = (f32[2,2,32,128]{3,2,1,0:T(8,128)S(1)}, f32[2,2,32,128]{3,2,1,0:T(8,128)S(1)}, u32[]{:S(2)}, u32[]{:S(2)}) collective-permute-start(f32[2,2,32,128]{3,2,1,0:T(8,128)S(1)} %bitcast.383), channel_id=1, source_target_pairs={{0,16},{8,24},{16,32},{24,40},{32,48},{40,56},{48,64},{56,72},{64,... | collective-permute-start | bytes 196616 | tf_op jit(solution)/shard_map/ppermute | solution.py:12
  399.5 10.8 %collective-permute-start.35 = (f32[2,2,32,128]{3,2,1,0:T(8,128)S(1)}, f32[2,2,32,128]{3,2,1,0:T(8,128)S(1)}, u32[]{:S(2)}, u32[]{:S(2)}) collective-permute-start(f32[2,2,32,128]{3,2,1,0:T(8,128)S(1)} %bitcast.382), channel_id=1, source_target_pairs={{0,8},{8,16},{16,24},{24,32},{32,40},{40,48},{48,56},{56,64},{64,7... | collective-permute-start | bytes 196616 | tf_op jit(solution)/shard_map/ppermute | solution.py:12
  408.9 9.0 %collective-permute-start.31 = (f32[2,2,32,128]{3,2,1,0:T(8,128)S(1)}, f32[2,2,32,128]{3,2,1,0:T(8,128)S(1)}, u32[]{:S(2)}, u32[]{:S(2)}) collective-permute-start(f32[2,2,32,128]{3,2,1,0:T(8,128)S(1)} %bitcast.378), channel_id=1, source_target_pairs={{32,0},{40,8},{48,16},{56,24},{64,32},{72,40},{80,48},{88,56},{96,... | collective-permute-start | bytes 196616 | tf_op jit(solution)/shard_map/ppermute | solution.py:12
  410.3 9.0 %collective-permute-start.30 = (f32[2,2,32,128]{3,2,1,0:T(8,128)S(1)}, f32[2,2,32,128]{3,2,1,0:T(8,128)S(1)}, u32[]{:S(2)}, u32[]{:S(2)}) collective-permute-start(f32[2,2,32,128]{3,2,1,0:T(8,128)S(1)} %bitcast.377), channel_id=1, source_target_pairs={{40,0},{48,8},{56,16},{64,24},{72,32},{80,40},{88,48},{96,56},{104... | collective-permute-start | bytes 196616 | tf_op jit(solution)/shard_map/ppermute | solution.py:12
  411.6 12.1 %collective-permute-start.29 = (f32[2,2,32,128]{3,2,1,0:T(8,128)S(1)}, f32[2,2,32,128]{3,2,1,0:T(8,128)S(1)}, u32[]{:S(2)}, u32[]{:S(2)}) collective-permute-start(f32[2,2,32,128]{3,2,1,0:T(8,128)S(1)} %bitcast.376), channel_id=1, source_target_pairs={{48,0},{56,8},{64,16},{72,24},{80,32},{88,40},{96,48},{104,56},{11... | collective-permute-start | bytes 196616 | tf_op jit(solution)/shard_map/ppermute | solution.py:12
  412.9 12.3 %collective-permute-start.28 = (f32[2,2,32,128]{3,2,1,0:T(8,128)S(1)}, f32[2,2,32,128]{3,2,1,0:T(8,128)S(1)}, u32[]{:S(2)}, u32[]{:S(2)}) collective-permute-start(f32[2,2,32,128]{3,2,1,0:T(8,128)S(1)} %bitcast.375), channel_id=1, source_target_pairs={{56,0},{64,8},{72,16},{80,24},{88,32},{96,40},{104,48},{112,56},{1... | collective-permute-start | bytes 196616 | tf_op jit(solution)/shard_map/ppermute | solution.py:12
  426.5 236.5 %all-reduce.11.cloned.1.call-start = ((), (), s32[]{:S(2)}) async-start(), calls=%async_computation.6 | async-start | bytes 524288
  534.8 16.8 %collective-permute-start.55 = (f32[1,2,32,128]{3,2,1,0:T(8,128)S(1)}, f32[1,2,32,128]{3,2,1,0:T(8,128)S(1)}, u32[]{:S(2)}, u32[]{:S(2)}) collective-permute-start(f32[1,2,32,128]{3,2,1,0:T(8,128)S(1)} %get-tuple-element.21), channel_id=1, source_target_pairs={{0,56},{8,64},{16,72},{24,80},{32,88},{40,96},{48,104},{56,112},{6... | collective-permute-start | bytes 98312 | tf_op jit(solution)/shard_map/ppermute | solution.py:12
  536.1 19.2 %collective-permute-start.54 = (f32[1,2,32,128]{3,2,1,0:T(8,128)S(1)}, f32[1,2,32,128]{3,2,1,0:T(8,128)S(1)}, u32[]{:S(2)}, u32[]{:S(2)}) collective-permute-start(f32[1,2,32,128]{3,2,1,0:T(8,128)S(1)} %get-tuple-element.22), channel_id=1, source_target_pairs={{0,48},{8,56},{16,64},{24,72},{32,80},{40,88},{48,96},{56,104},{64... | collective-permute-start | bytes 98312 | tf_op jit(solution)/shard_map/ppermute | solution.py:12
  540.3 19.3 %collective-permute-start.53 = (f32[1,2,32,128]{3,2,1,0:T(8,128)S(1)}, f32[1,2,32,128]{3,2,1,0:T(8,128)S(1)}, u32[]{:S(2)}, u32[]{:S(2)}) collective-permute-start(f32[1,2,32,128]{3,2,1,0:T(8,128)S(1)} %get-tuple-element.23), channel_id=1, source_target_pairs={{0,40},{8,48},{16,56},{24,64},{32,72},{40,80},{48,88},{56,96},{64,... | collective-permute-start | bytes 98312 | tf_op jit(solution)/shard_map/ppermute | solution.py:12
  545.7 15.9 %collective-permute-start.52 = (f32[1,2,32,128]{3,2,1,0:T(8,128)S(1)}, f32[1,2,32,128]{3,2,1,0:T(8,128)S(1)}, u32[]{:S(2)}, u32[]{:S(2)}) collective-permute-start(f32[1,2,32,128]{3,2,1,0:T(8,128)S(1)} %get-tuple-element.24), channel_id=1, source_target_pairs={{0,32},{8,40},{16,48},{24,56},{32,64},{40,72},{48,80},{56,88},{64,... | collective-permute-start | bytes 98312 | tf_op jit(solution)/shard_map/ppermute | solution.py:12
  549.8 13.6 %collective-permute-start.51 = (f32[1,2,32,128]{3,2,1,0:T(8,128)S(1)}, f32[1,2,32,128]{3,2,1,0:T(8,128)S(1)}, u32[]{:S(2)}, u32[]{:S(2)}) collective-permute-start(f32[1,2,32,128]{3,2,1,0:T(8,128)S(1)} %get-tuple-element.25), channel_id=1, source_target_pairs={{0,24},{8,32},{16,40},{24,48},{32,56},{40,64},{48,72},{56,80},{64,... | collective-permute-start | bytes 98312 | tf_op jit(solution)/shard_map/ppermute | solution.py:12
  551.6 13.2 %collective-permute-start.50 = (f32[1,2,32,128]{3,2,1,0:T(8,128)S(1)}, f32[1,2,32,128]{3,2,1,0:T(8,128)S(1)}, u32[]{:S(2)}, u32[]{:S(2)}) collective-permute-start(f32[1,2,32,128]{3,2,1,0:T(8,128)S(1)} %get-tuple-element.26), channel_id=1, source_target_pairs={{0,16},{8,24},{16,32},{24,40},{32,48},{40,56},{48,64},{56,72},{64,... | collective-permute-start | bytes 98312 | tf_op jit(solution)/shard_map/ppermute | solution.py:12
  555.3 10.8 %collective-permute-start.49 = (f32[1,2,32,128]{3,2,1,0:T(8,128)S(1)}, f32[1,2,32,128]{3,2,1,0:T(8,128)S(1)}, u32[]{:S(2)}, u32[]{:S(2)}) collective-permute-start(f32[1,2,32,128]{3,2,1,0:T(8,128)S(1)} %get-tuple-element.27), channel_id=1, source_target_pairs={{0,8},{8,16},{16,24},{24,32},{32,40},{40,48},{48,56},{56,64},{64,7... | collective-permute-start | bytes 98312 | tf_op jit(solution)/shard_map/ppermute | solution.py:12
  566.1 8.6 %collective-permute-start.44 = (f32[1,2,32,128]{3,2,1,0:T(8,128)S(1)}, f32[1,2,32,128]{3,2,1,0:T(8,128)S(1)}, u32[]{:S(2)}, u32[]{:S(2)}) collective-permute-start(f32[1,2,32,128]{3,2,1,0:T(8,128)S(1)} %get-tuple-element.32), channel_id=1, source_target_pairs={{40,0},{48,8},{56,16},{64,24},{72,32},{80,40},{88,48},{96,56},{104... | collective-permute-start | bytes 98312 | tf_op jit(solution)/shard_map/ppermute | solution.py:12
  567.4 11.5 %collective-permute-start.43 = (f32[1,2,32,128]{3,2,1,0:T(8,128)S(1)}, f32[1,2,32,128]{3,2,1,0:T(8,128)S(1)}, u32[]{:S(2)}, u32[]{:S(2)}) collective-permute-start(f32[1,2,32,128]{3,2,1,0:T(8,128)S(1)} %get-tuple-element.33), channel_id=1, source_target_pairs={{48,0},{56,8},{64,16},{72,24},{80,32},{88,40},{96,48},{104,56},{11... | collective-permute-start | bytes 98312 | tf_op jit(solution)/shard_map/ppermute | solution.py:12
  568.7 11.6 %collective-permute-start.42 = (f32[1,2,32,128]{3,2,1,0:T(8,128)S(1)}, f32[1,2,32,128]{3,2,1,0:T(8,128)S(1)}, u32[]{:S(2)}, u32[]{:S(2)}) collective-permute-start(f32[1,2,32,128]{3,2,1,0:T(8,128)S(1)} %get-tuple-element.20), channel_id=1, source_target_pairs={{56,0},{64,8},{72,16},{80,24},{88,32},{96,40},{104,48},{112,56},{1... | collective-permute-start | bytes 98312 | tf_op jit(solution)/shard_map/ppermute | solution.py:12
  (19 other events, 335.9 us)
Sparse Core Ops, SparseCore 0:
  85.4 44.6 reduce-scatter.2
  204.2 42.9 reduce-scatter.4
  274.4 76.6 all-reduce.6
  426.6 81.1 all-reduce.8
  581.8 81.1 all-reduce.10
where the time goes:
time: 673 us; the launch traced here: 671 us
  waiting for transfers between devices  366 us (54%)
  starting transfers between devices  142 us (21%)
  blocking collectives  126 us (19%)
  between operations  14.9 us (2%)
  local copies, waits for them, and re-layouts  11.1 us (2%)
  matrix products  8.02 us (1%)
    unnamed x8, waiting for transfers between devices  236 us
    ppermute x56, starting transfers between devices, from_behind(): lax.ppermute(value, axis, [(source, source + steps) for source in range(l...  142 us
    reduce_scatter x2, waiting for transfers between devices, local(): lax.psum_scatter(partial_value, 'cols', scatter_dimension=1, tiled=True)  87.7 us
    all_gather x3, blocking collectives, full_rows(): return lax.all_gather(piece, 'cols', axis=1, tiled=True)  76.1 us
    all_gather x2, blocking collectives, local(): whole_block = lax.all_gather(own_share, 'cols', axis=1, tiled=True)  49.7 us
    ppermute x56, waiting for transfers between devices, from_behind(): lax.ppermute(value, axis, [(source, source + steps) for source in range(l...  42.7 us
  transfers between devices with their start and end apart: 61, of which 21 were waited for; matrix products, arithmetic and copies ran while one was open for 1% of the time, Pallas kernels for 0%

commit v1 on v0

--- a/solution.py
+++ b/solution.py
@@ -80,7 +80,9 @@
         )
         own_share = lax.psum_scatter(partial_value, "cols", scatter_dimension=1, tiled=True)
         if height > 0:
-            whole_block = lax.all_gather(own_share, "cols", axis=1, tiled=True)
+            whole_block = jnp.concatenate(
+                lax.all_to_all(jnp.stack([own_share] * lax.axis_size("cols")), "cols", 0, 0), axis=1
+            )
         solution[height] = own_share
         if height > 0:
             term_set = jnp.einsum(

time: 673 us -> 650 us (0.966)
  blocking collectives: 126 us -> 76.1 us
  waiting for transfers between devices: 366 us -> 382 us
  starting transfers between devices: 142 us -> 151 us
    all_gather x2 -> x0, blocking collectives: 49.7 us -> none  [local(): whole_block = lax.all_gather(own_share, 'cols', axis=1, tiled=True)]
    all_to_all x0 -> x2, waiting for transfers between devices: none -> 20.7 us  [local(): lax.all_to_all(jnp.stack([own_share] * lax.axis_size('cols')), 'cols', 0, 0)]
    all_to_all x0 -> x2, starting transfers between devices: none -> 8.32 us  [local(): lax.all_to_all(jnp.stack([own_share] * lax.axis_size('cols')), 'cols', 0, 0)]
  transfers between devices with their start and end apart: 61 -> 63, of which waited for: 21 -> 23; matrix products, arithmetic and copies ran while one was open for 1% -> 1% of each run, Pallas kernels for 0% -> 0%
where the time goes in v1:
time: 650 us; the launch traced here: 647 us
  waiting for transfers between devices  382 us (59%)
  starting transfers between devices  151 us (23%)
  blocking collectives  76.1 us (12%)
  between operations  14.9 us (2%)
  local copies, waits for them, and re-layouts  12.7 us (2%)
  matrix products  8 us (1%)
    unnamed x8, waiting for transfers between devices  231 us
    ppermute x56, starting transfers between devices, from_behind(): lax.ppermute(value, axis, [(source, source + steps) for source in range(l...  142 us
    reduce_scatter x2, waiting for transfers between devices, local(): lax.psum_scatter(partial_value, 'cols', scatter_dimension=1, tiled=True)  87.7 us
    all_gather x3, blocking collectives, full_rows(): return lax.all_gather(piece, 'cols', axis=1, tiled=True)  76.1 us
    ppermute x56, waiting for transfers between devices, from_behind(): lax.ppermute(value, axis, [(source, source + steps) for source in range(l...  42.7 us
    all_to_all x2, waiting for transfers between devices, local(): lax.all_to_all(jnp.stack([own_share] * lax.axis_size('cols')), 'cols', 0, 0)  20.7 us
  transfers between devices with their start and end apart: 63, of which 23 were waited for; matrix products, arithmetic and copies ran while one was open for 1% of the time, Pallas kernels for 0%

profile of v1, /device:TPU:2, one launch (start us, length us, event | category | flops | bytes accessed | tf_op | source)
XLA Modules:
  0.0 647.3 jit_solution(9715259903519983221)
XLA Ops:
  7.3 26.5 %all-gather = f32[1,2,256,128]{3,2,1,0:T(8,128)S(1)} all-gather(f32[1,2,32,128]{3,2,1,0:T(8,128)S(1)} %slice-done), channel_id=2, replica_groups=mesh['rows'=64,'cols'=8] {'cols'}, dimensions={2}, use_global_device_ids=true | all-gather | bytes 294912 | tf_op jit(solution)/shard_map/all_gather | solution.py:39
  35.4 4.9 collective-permute-start.1
  40.2 6.1 collective-permute-start.2
  46.4 4.8 collective-permute-start.3
  52.7 4.0 collective-permute-start.5
  56.8 4.5 collective-permute-start.6
  61.3 1.9 collective-permute-start.7
  63.2 1.9 collective-permute-start.8
  71.8 3.7 collective-permute-done.10
  77.1 4.2 collective-permute-done.12
  85.4 44.6 %reduce-scatter.3.cloned.1.call-done = f32[2,32,128]{2,1,0:T(8,128)} async-done(((f32[2,256,128]{2,1,0:T(8,128)}), f32[2,32,128]{2,1,0:T(8,128)}) %reduce-scatter.3.cloned.1.call-update) | async-done | bytes 32784 | tf_op jit(solution)/shard_map/reduce_scatter | solution.py:60
  130.8 24.8 %all_gather.10 = f32[2,256,128]{2,1,0:T(8,128)S(1)} all-gather(f32[2,32,128]{2,1,0:T(8,128)S(1)} %bitcast_subtract_fusion), channel_id=1, replica_groups=mesh['rows'=64,'cols'=8] {'cols'}, dimensions={1}, use_global_device_ids=true | all-gather | bytes 294912 | tf_op jit(solution)/shard_map/all_gather | solution.py:39
  157.2 4.2 collective-permute-start.15
  161.4 5.4 collective-permute-start.16
  166.8 4.1 collective-permute-start.17
  172.7 3.8 collective-permute-start.19
  176.5 4.2 collective-permute-start.20
  180.7 1.9 collective-permute-start.21
  182.7 1.9 collective-permute-start.22
  191.2 3.0 collective-permute-done.24
  195.9 4.2 collective-permute-done.26
  204.1 43.1 %reduce-scatter.5.cloned.1.call-done = f32[2,32,128]{2,1,0:T(8,128)} async-done(((f32[2,256,128]{2,1,0:T(8,128)}), f32[2,32,128]{2,1,0:T(8,128)}) %reduce-scatter.5.cloned.1.call-update) | async-done | bytes 32784 | tf_op jit(solution)/shard_map/reduce_scatter | solution.py:60
  248.0 24.8 %all_gather.11 = f32[2,256,128]{2,1,0:T(8,128)S(1)} all-gather(f32[2,32,128]{2,1,0:T(8,128)S(1)} %bitcast_subtract_fusion.1), channel_id=1, replica_groups=mesh['rows'=64,'cols'=8] {'cols'}, dimensions={1}, use_global_device_ids=true | all-gather | bytes 294912 | tf_op jit(solution)/shard_map/all_gather | solution.py:39
  276.2 74.9 %all-reduce.7.cloned.1.call-done = f32[2,256,128]{2,0,1:T(2,128)} async-done(((f32[2,256,128]{2,0,1:T(2,128)}), f32[2,256,128]{2,0,1:T(2,128)}) %all-reduce.7.cloned.1.call-update) | async-done | bytes 262160
  352.7 4.2 all-to-all-start
  357.1 10.2 %all-to-all-done = f32[8,2,32,128]{3,2,1,0:T(8,128)S(1)} async-done(((f32[8,2,32,128]{3,2,1,0:T(8,128)}), f32[8,2,32,128]{3,2,1,0:T(8,128)S(1)}, u32[]{:S(2)}, u32[]{:S(2)}) %all-to-all-start) | async-done | bytes 262176 | tf_op jit(solution)/shard_map/all_to_all | solution.py:84
  370.8 4.2 collective-permute-start.40
  375.0 5.3 collective-permute-start.39
  380.4 4.1 collective-permute-start.38
  386.3 3.7 collective-permute-start.36
  390.0 4.3 collective-permute-start.35
  394.3 1.9 collective-permute-start.34
  396.3 1.9 collective-permute-start.33
  404.7 3.8 collective-permute-done.31
  409.8 4.4 collective-permute-done.29
  417.1 79.0 %all-reduce.9.cloned.1.call-done = f32[2,256,128]{2,0,1:T(2,128)} async-done(((f32[2,256,128]{2,0,1:T(2,128)}), f32[2,256,128]{2,0,1:T(2,128)}) %all-reduce.9.cloned.1.call-update) | async-done | bytes 262160
  497.6 4.2 all-to-all-start.1
  501.8 10.4 %all-to-all-done.1 = f32[8,2,32,128]{3,2,1,0:T(8,128)S(1)} async-done(((f32[8,2,32,128]{3,2,1,0:T(8,128)}), f32[8,2,32,128]{3,2,1,0:T(8,128)S(1)}, u32[]{:S(2)}, u32[]{:S(2)}) %all-to-all-start.1) | async-done | bytes 262176 | tf_op jit(solution)/shard_map/all_to_all | solution.py:84
  514.8 4.2 collective-permute-start.54
  519.0 5.4 collective-permute-start.53
  524.4 4.1 collective-permute-start.52
  530.3 3.7 collective-permute-start.50
  534.0 4.3 collective-permute-start.49
  538.3 1.9 collective-permute-start.48
  540.2 1.9 collective-permute-start.47
  548.7 3.1 collective-permute-done.45
  553.4 4.2 collective-permute-done.43
  561.9 77.4 %all-reduce.11.cloned.1.call-done = f32[2,256,128]{2,0,1:T(2,128)} async-done(((f32[2,256,128]{2,0,1:T(2,128)}), f32[2,256,128]{2,0,1:T(2,128)}) %all-reduce.11.cloned.1.call-update) | async-done | bytes 262160
  (182 shorter events, 73.1 us)
Async XLA Ops:
  6.5 123.5 %reduce-scatter.3.cloned.1.call-start = ((), (), s32[]{:S(2)}) async-start(), calls=%async_computation.4 | async-start | bytes 294912 | tf_op jit(solution)/shard_map/reduce_scatter | solution.py:60
  34.1 18.7 %collective-permute-start = (f32[2,32,128]{2,1,0:T(8,128)S(1)}, f32[2,32,128]{2,1,0:T(8,128)S(1)}, u32[]{:S(2)}, u32[]{:S(2)}) collective-permute-start(f32[2,32,128]{2,1,0:T(8,128)S(1)} %fusion.12), channel_id=1, source_target_pairs={{0,56},{8,64},{16,72},{24,80},{32,88},{40,96},{48,104},{56,112},{6... | collective-permute-start | bytes 98312 | tf_op jit(solution)/shard_map/ppermute | solution.py:12
  35.4 21.4 %collective-permute-start.1 = (f32[2,32,128]{2,1,0:T(8,128)S(1)}, f32[2,32,128]{2,1,0:T(8,128)S(1)}, u32[]{:S(2)}, u32[]{:S(2)}) collective-permute-start(f32[2,32,128]{2,1,0:T(8,128)S(1)} %fusion.12), channel_id=1, source_target_pairs={{0,48},{8,56},{16,64},{24,72},{32,80},{40,88},{48,96},{56,104},{64... | collective-permute-start | bytes 98312 | tf_op jit(solution)/shard_map/ppermute | solution.py:12
  40.2 21.0 %collective-permute-start.2 = (f32[2,32,128]{2,1,0:T(8,128)S(1)}, f32[2,32,128]{2,1,0:T(8,128)S(1)}, u32[]{:S(2)}, u32[]{:S(2)}) collective-permute-start(f32[2,32,128]{2,1,0:T(8,128)S(1)} %fusion.12), channel_id=1, source_target_pairs={{0,40},{8,48},{16,56},{24,64},{32,72},{40,80},{48,88},{56,96},{64,... | collective-permute-start | bytes 98312 | tf_op jit(solution)/shard_map/ppermute | solution.py:12
  46.4 16.9 %collective-permute-start.3 = (f32[2,32,128]{2,1,0:T(8,128)S(1)}, f32[2,32,128]{2,1,0:T(8,128)S(1)}, u32[]{:S(2)}, u32[]{:S(2)}) collective-permute-start(f32[2,32,128]{2,1,0:T(8,128)S(1)} %fusion.12), channel_id=1, source_target_pairs={{0,32},{8,40},{16,48},{24,56},{32,64},{40,72},{48,80},{56,88},{64,... | collective-permute-start | bytes 98312 | tf_op jit(solution)/shard_map/ppermute | solution.py:12
  51.2 14.0 %collective-permute-start.4 = (f32[2,32,128]{2,1,0:T(8,128)S(1)}, f32[2,32,128]{2,1,0:T(8,128)S(1)}, u32[]{:S(2)}, u32[]{:S(2)}) collective-permute-start(f32[2,32,128]{2,1,0:T(8,128)S(1)} %fusion.12), channel_id=1, source_target_pairs={{0,24},{8,32},{16,40},{24,48},{32,56},{40,64},{48,72},{56,80},{64,... | collective-permute-start | bytes 98312 | tf_op jit(solution)/shard_map/ppermute | solution.py:12
  52.7 13.8 %collective-permute-start.5 = (f32[2,32,128]{2,1,0:T(8,128)S(1)}, f32[2,32,128]{2,1,0:T(8,128)S(1)}, u32[]{:S(2)}, u32[]{:S(2)}) collective-permute-start(f32[2,32,128]{2,1,0:T(8,128)S(1)} %fusion.12), channel_id=1, source_target_pairs={{0,16},{8,24},{16,32},{24,40},{32,48},{40,56},{48,64},{56,72},{64,... | collective-permute-start | bytes 98312 | tf_op jit(solution)/shard_map/ppermute | solution.py:12
  56.8 11.0 %collective-permute-start.6 = (f32[2,32,128]{2,1,0:T(8,128)S(1)}, f32[2,32,128]{2,1,0:T(8,128)S(1)}, u32[]{:S(2)}, u32[]{:S(2)}) collective-permute-start(f32[2,32,128]{2,1,0:T(8,128)S(1)} %fusion.12), channel_id=1, source_target_pairs={{0,8},{8,16},{16,24},{24,32},{32,40},{40,48},{48,56},{56,64},{64,7... | collective-permute-start | bytes 98312 | tf_op jit(solution)/shard_map/ppermute | solution.py:12
  66.5 9.0 %collective-permute-start.10 = (f32[2,32,128]{2,1,0:T(8,128)S(1)}, f32[2,32,128]{2,1,0:T(8,128)S(1)}, u32[]{:S(2)}, u32[]{:S(2)}) collective-permute-start(f32[2,32,128]{2,1,0:T(8,128)S(1)} %fusion.12), channel_id=1, source_target_pairs={{32,0},{40,8},{48,16},{56,24},{64,32},{72,40},{80,48},{88,56},{96,... | collective-permute-start | bytes 98312 | tf_op jit(solution)/shard_map/ppermute | solution.py:12
  67.8 9.3 %collective-permute-start.11 = (f32[2,32,128]{2,1,0:T(8,128)S(1)}, f32[2,32,128]{2,1,0:T(8,128)S(1)}, u32[]{:S(2)}, u32[]{:S(2)}) collective-permute-start(f32[2,32,128]{2,1,0:T(8,128)S(1)} %fusion.12), channel_id=1, source_target_pairs={{40,0},{48,8},{56,16},{64,24},{72,32},{80,40},{88,48},{96,56},{104... | collective-permute-start | bytes 98312 | tf_op jit(solution)/shard_map/ppermute | solution.py:12
  69.2 12.2 %collective-permute-start.12 = (f32[2,32,128]{2,1,0:T(8,128)S(1)}, f32[2,32,128]{2,1,0:T(8,128)S(1)}, u32[]{:S(2)}, u32[]{:S(2)}) collective-permute-start(f32[2,32,128]{2,1,0:T(8,128)S(1)} %fusion.12), channel_id=1, source_target_pairs={{48,0},{56,8},{64,16},{72,24},{80,32},{88,40},{96,48},{104,56},{11... | collective-permute-start | bytes 98312 | tf_op jit(solution)/shard_map/ppermute | solution.py:12
  70.5 12.3 %collective-permute-start.13 = (f32[2,32,128]{2,1,0:T(8,128)S(1)}, f32[2,32,128]{2,1,0:T(8,128)S(1)}, u32[]{:S(2)}, u32[]{:S(2)}) collective-permute-start(f32[2,32,128]{2,1,0:T(8,128)S(1)} %fusion.12), channel_id=1, source_target_pairs={{56,0},{64,8},{72,16},{80,24},{88,32},{96,40},{104,48},{112,56},{1... | collective-permute-start | bytes 98312 | tf_op jit(solution)/shard_map/ppermute | solution.py:12
  85.2 162.0 %reduce-scatter.5.cloned.1.call-start = ((), (), s32[]{:S(2)}) async-start(), calls=%async_computation.5 | async-start | bytes 294912 | tf_op jit(solution)/shard_map/reduce_scatter | solution.py:60
  155.9 16.8 %collective-permute-start.14 = (f32[2,32,128]{2,1,0:T(8,128)S(1)}, f32[2,32,128]{2,1,0:T(8,128)S(1)}, u32[]{:S(2)}, u32[]{:S(2)}) collective-permute-start(f32[2,32,128]{2,1,0:T(8,128)S(1)} %bitcast.374), channel_id=1, source_target_pairs={{0,56},{8,64},{16,72},{24,80},{32,88},{40,96},{48,104},{56,112},{6... | collective-permute-start | bytes 98312 | tf_op jit(solution)/shard_map/ppermute | solution.py:12
  157.2 19.3 %collective-permute-start.15 = (f32[2,32,128]{2,1,0:T(8,128)S(1)}, f32[2,32,128]{2,1,0:T(8,128)S(1)}, u32[]{:S(2)}, u32[]{:S(2)}) collective-permute-start(f32[2,32,128]{2,1,0:T(8,128)S(1)} %bitcast.375), channel_id=1, source_target_pairs={{0,48},{8,56},{16,64},{24,72},{32,80},{40,88},{48,96},{56,104},{64... | collective-permute-start | bytes 98312 | tf_op jit(solution)/shard_map/ppermute | solution.py:12
  161.4 19.3 %collective-permute-start.16 = (f32[2,32,128]{2,1,0:T(8,128)S(1)}, f32[2,32,128]{2,1,0:T(8,128)S(1)}, u32[]{:S(2)}, u32[]{:S(2)}) collective-permute-start(f32[2,32,128]{2,1,0:T(8,128)S(1)} %bitcast.376), channel_id=1, source_target_pairs={{0,40},{8,48},{16,56},{24,64},{32,72},{40,80},{48,88},{56,96},{64,... | collective-permute-start | bytes 98312 | tf_op jit(solution)/shard_map/ppermute | solution.py:12
  166.8 15.9 %collective-permute-start.17 = (f32[2,32,128]{2,1,0:T(8,128)S(1)}, f32[2,32,128]{2,1,0:T(8,128)S(1)}, u32[]{:S(2)}, u32[]{:S(2)}) collective-permute-start(f32[2,32,128]{2,1,0:T(8,128)S(1)} %bitcast.377), channel_id=1, source_target_pairs={{0,32},{8,40},{16,48},{24,56},{32,64},{40,72},{48,80},{56,88},{64,... | collective-permute-start | bytes 98312 | tf_op jit(solution)/shard_map/ppermute | solution.py:12
  170.9 13.7 %collective-permute-start.18 = (f32[2,32,128]{2,1,0:T(8,128)S(1)}, f32[2,32,128]{2,1,0:T(8,128)S(1)}, u32[]{:S(2)}, u32[]{:S(2)}) collective-permute-start(f32[2,32,128]{2,1,0:T(8,128)S(1)} %bitcast.378), channel_id=1, source_target_pairs={{0,24},{8,32},{16,40},{24,48},{32,56},{40,64},{48,72},{56,80},{64,... | collective-permute-start | bytes 98312 | tf_op jit(solution)/shard_map/ppermute | solution.py:12
  172.7 13.2 %collective-permute-start.19 = (f32[2,32,128]{2,1,0:T(8,128)S(1)}, f32[2,32,128]{2,1,0:T(8,128)S(1)}, u32[]{:S(2)}, u32[]{:S(2)}) collective-permute-start(f32[2,32,128]{2,1,0:T(8,128)S(1)} %bitcast.379), channel_id=1, source_target_pairs={{0,16},{8,24},{16,32},{24,40},{32,48},{40,56},{48,64},{56,72},{64,... | collective-permute-start | bytes 98312 | tf_op jit(solution)/shard_map/ppermute | solution.py:12
  176.5 10.7 %collective-permute-start.20 = (f32[2,32,128]{2,1,0:T(8,128)S(1)}, f32[2,32,128]{2,1,0:T(8,128)S(1)}, u32[]{:S(2)}, u32[]{:S(2)}) collective-permute-start(f32[2,32,128]{2,1,0:T(8,128)S(1)} %bitcast.380), channel_id=1, source_target_pairs={{0,8},{8,16},{16,24},{24,32},{32,40},{40,48},{48,56},{56,64},{64,7... | collective-permute-start | bytes 98312 | tf_op jit(solution)/shard_map/ppermute | solution.py:12
  188.6 11.5 %collective-permute-start.26 = (f32[2,32,128]{2,1,0:T(8,128)S(1)}, f32[2,32,128]{2,1,0:T(8,128)S(1)}, u32[]{:S(2)}, u32[]{:S(2)}) collective-permute-start(f32[2,32,128]{2,1,0:T(8,128)S(1)} %bitcast.386), channel_id=1, source_target_pairs={{48,0},{56,8},{64,16},{72,24},{80,32},{88,40},{96,48},{104,56},{11... | collective-permute-start | bytes 98312 | tf_op jit(solution)/shard_map/ppermute | solution.py:12
  189.9 11.6 %collective-permute-start.27 = (f32[2,32,128]{2,1,0:T(8,128)S(1)}, f32[2,32,128]{2,1,0:T(8,128)S(1)}, u32[]{:S(2)}, u32[]{:S(2)}) collective-permute-start(f32[2,32,128]{2,1,0:T(8,128)S(1)} %bitcast.387), channel_id=1, source_target_pairs={{56,0},{64,8},{72,16},{80,24},{88,32},{96,40},{104,48},{112,56},{1... | collective-permute-start | bytes 98312 | tf_op jit(solution)/shard_map/ppermute | solution.py:12
  204.1 147.1 %all-reduce.7.cloned.1.call-start = ((), (), s32[]{:S(2)}) async-start(), calls=%async_computation.6 | async-start | bytes 524288
  352.7 14.6 %all-to-all-start = ((f32[8,2,32,128]{3,2,1,0:T(8,128)}), f32[8,2,32,128]{3,2,1,0:T(8,128)S(1)}, u32[]{:S(2)}, u32[]{:S(2)}) async-start(f32[8,2,32,128]{3,2,1,0:T(8,128)} %stack.174), calls=%async_computation.2 | async-start | bytes 524288 | tf_op jit(solution)/shard_map/all_to_all | solution.py:84
  356.8 139.2 %all-reduce.9.cloned.1.call-start = ((), (), s32[]{:S(2)}) async-start(), calls=%async_computation.7 | async-start | bytes 524288
  369.5 16.8 %collective-permute-start.41 = (f32[2,2,32,128]{3,2,1,0:T(8,128)S(1)}, f32[2,2,32,128]{3,2,1,0:T(8,128)S(1)}, u32[]{:S(2)}, u32[]{:S(2)}) collective-permute-start(f32[2,2,32,128]{3,2,1,0:T(8,128)S(1)} %bitcast.402), channel_id=1, source_target_pairs={{0,56},{8,64},{16,72},{24,80},{32,88},{40,96},{48,104},{56,112},{6... | collective-permute-start | bytes 196616 | tf_op jit(solution)/shard_map/ppermute | solution.py:12
  370.8 19.2 %collective-permute-start.40 = (f32[2,2,32,128]{3,2,1,0:T(8,128)S(1)}, f32[2,2,32,128]{3,2,1,0:T(8,128)S(1)}, u32[]{:S(2)}, u32[]{:S(2)}) collective-permute-start(f32[2,2,32,128]{3,2,1,0:T(8,128)S(1)} %bitcast.401), channel_id=1, source_target_pairs={{0,48},{8,56},{16,64},{24,72},{32,80},{40,88},{48,96},{56,104},{64... | collective-permute-start | bytes 196616 | tf_op jit(solution)/shard_map/ppermute | solution.py:12
  375.0 19.3 %collective-permute-start.39 = (f32[2,2,32,128]{3,2,1,0:T(8,128)S(1)}, f32[2,2,32,128]{3,2,1,0:T(8,128)S(1)}, u32[]{:S(2)}, u32[]{:S(2)}) collective-permute-start(f32[2,2,32,128]{3,2,1,0:T(8,128)S(1)} %bitcast.400), channel_id=1, source_target_pairs={{0,40},{8,48},{16,56},{24,64},{32,72},{40,80},{48,88},{56,96},{64,... | collective-permute-start | bytes 196616 | tf_op jit(solution)/shard_map/ppermute | solution.py:12
  380.4 15.9 %collective-permute-start.38 = (f32[2,2,32,128]{3,2,1,0:T(8,128)S(1)}, f32[2,2,32,128]{3,2,1,0:T(8,128)S(1)}, u32[]{:S(2)}, u32[]{:S(2)}) collective-permute-start(f32[2,2,32,128]{3,2,1,0:T(8,128)S(1)} %bitcast.399), channel_id=1, source_target_pairs={{0,32},{8,40},{16,48},{24,56},{32,64},{40,72},{48,80},{56,88},{64,... | collective-permute-start | bytes 196616 | tf_op jit(solution)/shard_map/ppermute | solution.py:12
  384.5 13.6 %collective-permute-start.37 = (f32[2,2,32,128]{3,2,1,0:T(8,128)S(1)}, f32[2,2,32,128]{3,2,1,0:T(8,128)S(1)}, u32[]{:S(2)}, u32[]{:S(2)}) collective-permute-start(f32[2,2,32,128]{3,2,1,0:T(8,128)S(1)} %bitcast.398), channel_id=1, source_target_pairs={{0,24},{8,32},{16,40},{24,48},{32,56},{40,64},{48,72},{56,80},{64,... | collective-permute-start | bytes 196616 | tf_op jit(solution)/shard_map/ppermute | solution.py:12
  386.3 13.2 %collective-permute-start.36 = (f32[2,2,32,128]{3,2,1,0:T(8,128)S(1)}, f32[2,2,32,128]{3,2,1,0:T(8,128)S(1)}, u32[]{:S(2)}, u32[]{:S(2)}) collective-permute-start(f32[2,2,32,128]{3,2,1,0:T(8,128)S(1)} %bitcast.397), channel_id=1, source_target_pairs={{0,16},{8,24},{16,32},{24,40},{32,48},{40,56},{48,64},{56,72},{64,... | collective-permute-start | bytes 196616 | tf_op jit(solution)/shard_map/ppermute | solution.py:12
  390.0 10.8 %collective-permute-start.35 = (f32[2,2,32,128]{3,2,1,0:T(8,128)S(1)}, f32[2,2,32,128]{3,2,1,0:T(8,128)S(1)}, u32[]{:S(2)}, u32[]{:S(2)}) collective-permute-start(f32[2,2,32,128]{3,2,1,0:T(8,128)S(1)} %bitcast.396), channel_id=1, source_target_pairs={{0,8},{8,16},{16,24},{24,32},{32,40},{40,48},{48,56},{56,64},{64,7... | collective-permute-start | bytes 196616 | tf_op jit(solution)/shard_map/ppermute | solution.py:12
  399.5 9.0 %collective-permute-start.31 = (f32[2,2,32,128]{3,2,1,0:T(8,128)S(1)}, f32[2,2,32,128]{3,2,1,0:T(8,128)S(1)}, u32[]{:S(2)}, u32[]{:S(2)}) collective-permute-start(f32[2,2,32,128]{3,2,1,0:T(8,128)S(1)} %bitcast.392), channel_id=1, source_target_pairs={{32,0},{40,8},{48,16},{56,24},{64,32},{72,40},{80,48},{88,56},{96,... | collective-permute-start | bytes 196616 | tf_op jit(solution)/shard_map/ppermute | solution.py:12
  400.8 9.0 %collective-permute-start.30 = (f32[2,2,32,128]{3,2,1,0:T(8,128)S(1)}, f32[2,2,32,128]{3,2,1,0:T(8,128)S(1)}, u32[]{:S(2)}, u32[]{:S(2)}) collective-permute-start(f32[2,2,32,128]{3,2,1,0:T(8,128)S(1)} %bitcast.391), channel_id=1, source_target_pairs={{40,0},{48,8},{56,16},{64,24},{72,32},{80,40},{88,48},{96,56},{104... | collective-permute-start | bytes 196616 | tf_op jit(solution)/shard_map/ppermute | solution.py:12
  402.1 12.1 %collective-permute-start.29 = (f32[2,2,32,128]{3,2,1,0:T(8,128)S(1)}, f32[2,2,32,128]{3,2,1,0:T(8,128)S(1)}, u32[]{:S(2)}, u32[]{:S(2)}) collective-permute-start(f32[2,2,32,128]{3,2,1,0:T(8,128)S(1)} %bitcast.390), channel_id=1, source_target_pairs={{48,0},{56,8},{64,16},{72,24},{80,32},{88,40},{96,48},{104,56},{11... | collective-permute-start | bytes 196616 | tf_op jit(solution)/shard_map/ppermute | solution.py:12
  403.4 12.3 %collective-permute-start.28 = (f32[2,2,32,128]{3,2,1,0:T(8,128)S(1)}, f32[2,2,32,128]{3,2,1,0:T(8,128)S(1)}, u32[]{:S(2)}, u32[]{:S(2)}) collective-permute-start(f32[2,2,32,128]{3,2,1,0:T(8,128)S(1)} %bitcast.389), channel_id=1, source_target_pairs={{56,0},{64,8},{72,16},{80,24},{88,32},{96,40},{104,48},{112,56},{1... | collective-permute-start | bytes 196616 | tf_op jit(solution)/shard_map/ppermute | solution.py:12
  497.6 14.6 %all-to-all-start.1 = ((f32[8,2,32,128]{3,2,1,0:T(8,128)}), f32[8,2,32,128]{3,2,1,0:T(8,128)S(1)}, u32[]{:S(2)}, u32[]{:S(2)}) async-start(f32[8,2,32,128]{3,2,1,0:T(8,128)} %stack.175), calls=%async_computation.3 | async-start | bytes 524288 | tf_op jit(solution)/shard_map/all_to_all | solution.py:84
  501.7 137.6 %all-reduce.11.cloned.1.call-start = ((), (), s32[]{:S(2)}) async-start(), calls=%async_computation.8 | async-start | bytes 524288
  513.5 16.8 %collective-permute-start.55 = (f32[1,2,32,128]{3,2,1,0:T(8,128)S(1)}, f32[1,2,32,128]{3,2,1,0:T(8,128)S(1)}, u32[]{:S(2)}, u32[]{:S(2)}) collective-permute-start(f32[1,2,32,128]{3,2,1,0:T(8,128)S(1)} %get-tuple-element.21), channel_id=1, source_target_pairs={{0,56},{8,64},{16,72},{24,80},{32,88},{40,96},{48,104},{56,112},{6... | collective-permute-start | bytes 98312 | tf_op jit(solution)/shard_map/ppermute | solution.py:12
  514.8 19.2 %collective-permute-start.54 = (f32[1,2,32,128]{3,2,1,0:T(8,128)S(1)}, f32[1,2,32,128]{3,2,1,0:T(8,128)S(1)}, u32[]{:S(2)}, u32[]{:S(2)}) collective-permute-start(f32[1,2,32,128]{3,2,1,0:T(8,128)S(1)} %get-tuple-element.22), channel_id=1, source_target_pairs={{0,48},{8,56},{16,64},{24,72},{32,80},{40,88},{48,96},{56,104},{64... | collective-permute-start | bytes 98312 | tf_op jit(solution)/shard_map/ppermute | solution.py:12
  519.0 19.3 %collective-permute-start.53 = (f32[1,2,32,128]{3,2,1,0:T(8,128)S(1)}, f32[1,2,32,128]{3,2,1,0:T(8,128)S(1)}, u32[]{:S(2)}, u32[]{:S(2)}) collective-permute-start(f32[1,2,32,128]{3,2,1,0:T(8,128)S(1)} %get-tuple-element.23), channel_id=1, source_target_pairs={{0,40},{8,48},{16,56},{24,64},{32,72},{40,80},{48,88},{56,96},{64,... | collective-permute-start | bytes 98312 | tf_op jit(solution)/shard_map/ppermute | solution.py:12
  524.4 15.9 %collective-permute-start.52 = (f32[1,2,32,128]{3,2,1,0:T(8,128)S(1)}, f32[1,2,32,128]{3,2,1,0:T(8,128)S(1)}, u32[]{:S(2)}, u32[]{:S(2)}) collective-permute-start(f32[1,2,32,128]{3,2,1,0:T(8,128)S(1)} %get-tuple-element.24), channel_id=1, source_target_pairs={{0,32},{8,40},{16,48},{24,56},{32,64},{40,72},{48,80},{56,88},{64,... | collective-permute-start | bytes 98312 | tf_op jit(solution)/shard_map/ppermute | solution.py:12
  528.5 13.6 %collective-permute-start.51 = (f32[1,2,32,128]{3,2,1,0:T(8,128)S(1)}, f32[1,2,32,128]{3,2,1,0:T(8,128)S(1)}, u32[]{:S(2)}, u32[]{:S(2)}) collective-permute-start(f32[1,2,32,128]{3,2,1,0:T(8,128)S(1)} %get-tuple-element.25), channel_id=1, source_target_pairs={{0,24},{8,32},{16,40},{24,48},{32,56},{40,64},{48,72},{56,80},{64,... | collective-permute-start | bytes 98312 | tf_op jit(solution)/shard_map/ppermute | solution.py:12
  530.3 13.2 %collective-permute-start.50 = (f32[1,2,32,128]{3,2,1,0:T(8,128)S(1)}, f32[1,2,32,128]{3,2,1,0:T(8,128)S(1)}, u32[]{:S(2)}, u32[]{:S(2)}) collective-permute-start(f32[1,2,32,128]{3,2,1,0:T(8,128)S(1)} %get-tuple-element.26), channel_id=1, source_target_pairs={{0,16},{8,24},{16,32},{24,40},{32,48},{40,56},{48,64},{56,72},{64,... | collective-permute-start | bytes 98312 | tf_op jit(solution)/shard_map/ppermute | solution.py:12
  534.0 10.8 %collective-permute-start.49 = (f32[1,2,32,128]{3,2,1,0:T(8,128)S(1)}, f32[1,2,32,128]{3,2,1,0:T(8,128)S(1)}, u32[]{:S(2)}, u32[]{:S(2)}) collective-permute-start(f32[1,2,32,128]{3,2,1,0:T(8,128)S(1)} %get-tuple-element.27), channel_id=1, source_target_pairs={{0,8},{8,16},{16,24},{24,32},{32,40},{40,48},{48,56},{56,64},{64,7... | collective-permute-start | bytes 98312 | tf_op jit(solution)/shard_map/ppermute | solution.py:12
  544.8 8.6 %collective-permute-start.44 = (f32[1,2,32,128]{3,2,1,0:T(8,128)S(1)}, f32[1,2,32,128]{3,2,1,0:T(8,128)S(1)}, u32[]{:S(2)}, u32[]{:S(2)}) collective-permute-start(f32[1,2,32,128]{3,2,1,0:T(8,128)S(1)} %get-tuple-element.32), channel_id=1, source_target_pairs={{40,0},{48,8},{56,16},{64,24},{72,32},{80,40},{88,48},{96,56},{104... | collective-permute-start | bytes 98312 | tf_op jit(solution)/shard_map/ppermute | solution.py:12
  546.1 11.5 %collective-permute-start.43 = (f32[1,2,32,128]{3,2,1,0:T(8,128)S(1)}, f32[1,2,32,128]{3,2,1,0:T(8,128)S(1)}, u32[]{:S(2)}, u32[]{:S(2)}) collective-permute-start(f32[1,2,32,128]{3,2,1,0:T(8,128)S(1)} %get-tuple-element.33), channel_id=1, source_target_pairs={{48,0},{56,8},{64,16},{72,24},{80,32},{88,40},{96,48},{104,56},{11... | collective-permute-start | bytes 98312 | tf_op jit(solution)/shard_map/ppermute | solution.py:12
  547.4 11.6 %collective-permute-start.42 = (f32[1,2,32,128]{3,2,1,0:T(8,128)S(1)}, f32[1,2,32,128]{3,2,1,0:T(8,128)S(1)}, u32[]{:S(2)}, u32[]{:S(2)}) collective-permute-start(f32[1,2,32,128]{3,2,1,0:T(8,128)S(1)} %get-tuple-element.20), channel_id=1, source_target_pairs={{56,0},{64,8},{72,16},{80,24},{88,32},{96,40},{104,48},{112,56},{1... | collective-permute-start | bytes 98312 | tf_op jit(solution)/shard_map/ppermute | solution.py:12
  (21 other events, 352.9 us)
Sparse Core Ops, SparseCore 0:
  85.4 44.6 reduce-scatter.2
  204.2 42.9 reduce-scatter.4
  274.4 76.6 all-reduce.6
  417.2 78.8 all-reduce.8
  560.5 78.7 all-reduce.10
